TPU v7x, 256 devices: a whole 4x4x8 slice. The times are simulated.
256 devices in a mesh: req: 32 (over y, x, core), head: 8 (over z).
Axes of the slice: x: 4, y: 4, z: 8, core: 2. Of those that a mesh axis runs over, the one named last changes fastest.
Arguments:
- queries: bfloat16 [1024, 16384], P(('req', 'head')), may hold values from -15 to 15
- cache_keys: bfloat16 [8, 32768, 1024], P(None, 'req', 'head'), may hold values from -6 to 6
- cache_values: bfloat16 [8, 32768, 1024], P(None, 'req', 'head'), may hold values from -6 to 6
- tree_keys: bfloat16 [1024, 1024], P('req', 'head'), may hold values from -10 to 10
- tree_values: bfloat16 [1024, 1024], P('req', 'head'), may hold values from -6 to 6
- parents: int32 [8, 128], replicated, may hold values from -1 to 126, as said below
- tree_sizes: int32 [8], replicated, may hold values from 16 to 128
- cache_lens: int32 [8], replicated, may hold values from 2 to 32768
Outputs:
- attended: bfloat16 [1024, 16384], P('req', 'head')
Inputs may be any that keep to these rules, and one draw needn't show every extreme that they name: parents[a, 0] = -1 (the root); for node i >= 1, parents[a, i] is a node of 0 to i - 1.
All inputs are finite; a program needn't handle non-finite values.
Results may differ from a plain program's by a relative error of at most 0.003.
Values may be sent and summed in bfloat16 or wider, within the bound.
A program may use at most 128 MiB of HBM per device.

v0:
```python
import math
import jax
import jax.numpy as jnp
from jax import lax
from jax.sharding import Mesh
from jax.sharding import PartitionSpec as P

NH = 128
KVH = 8
HD = 128
negative_fill = -1e30


def ancestry(parents):
    node_count = parents.shape[1]
    node_ids = jnp.arange(node_count, dtype=jnp.int32)
    linked = jnp.logical_or(
        parents[:, :, None] == node_ids[None, None, :], node_ids[:, None] == node_ids[None, :]
    )
    reached = linked.astype(jnp.bfloat16)
    for doubling in range((node_count - 1).bit_length()):
        squared = jnp.einsum("aij,ajk->aik", reached, reached, preferred_element_type=jnp.float32)
        reached = jnp.minimum(squared, 1.0).astype(jnp.bfloat16)
    return reached


def body(
    queries, cache_keys, cache_values, tree_keys, tree_values, parents, tree_sizes, cache_lens
):
    group_size = NH // KVH
    softmax_scale = 1.0 / math.sqrt(HD)
    request = lax.axis_index("rh")
    quarter = lax.axis_index("rl")
    n_lo = lax.axis_size("rl")
    n_hi = lax.axis_size("rh")
    cache_block = cache_keys.shape[1]
    kv_local = cache_keys.shape[2] // HD
    heads_local = kv_local * group_size
    node_count = parents.shape[1]
    rows_owned = tree_keys.shape[0]
    by_head = lax.all_to_all(queries, "head", split_axis=1, concat_axis=0, tiled=True)
    query_block = lax.all_gather(by_head, "rl", axis=0, tiled=True)
    query_block = query_block.reshape(node_count, kv_local, group_size, HD)
    both = jnp.concatenate([cache_keys, cache_values], axis=2)
    mine = lax.all_to_all(both, "rh", split_axis=0, concat_axis=1, tiled=True)[0]
    mine = mine.reshape(n_hi, cache_block, 2, kv_local, HD)
    reached = ancestry(parents)
    ancestors = lax.dynamic_index_in_dim(reached, request, 0, keepdims=False)
    ancestors = lax.dynamic_slice_in_dim(ancestors, quarter * rows_owned, rows_owned, 1)
    live_tree_all = ancestors > 0.5
    length = lax.dynamic_index_in_dim(cache_lens, request, 0, keepdims=False)
    local_tree_keys = tree_keys.reshape(rows_owned, kv_local, HD)
    local_tree_values = tree_values.reshape(rows_owned, kv_local, HD)

    def one_group(s):
        block = s * n_lo + quarter
        positions = block * cache_block + jnp.arange(cache_block, dtype=jnp.int32)
        live_cache = positions < length
        live_tree = jnp.logical_and(live_tree_all, s == request)
        block_keys = mine[s, :, 0]
        block_values = mine[s, :, 1]
        cache_scores = (
            jnp.einsum(
                "igqd,pgd->igqp", query_block, block_keys, preferred_element_type=jnp.float32
            )
            * softmax_scale
        )
        cache_scores = jnp.where(live_cache[None, None, None, :], cache_scores, negative_fill)
        tree_scores = (
            jnp.einsum(
                "igqd,rgd->igqr", query_block, local_tree_keys, preferred_element_type=jnp.float32
            )
            * softmax_scale
        )
        tree_scores = jnp.where(live_tree[:, None, None, :], tree_scores, negative_fill)
        peaks = jnp.maximum(jnp.max(cache_scores, axis=3), jnp.max(tree_scores, axis=3))
        cache_weights = jnp.where(
            live_cache[None, None, None, :], jnp.exp(cache_scores - peaks[..., None]), 0.0
        )
        tree_weights = jnp.where(
            live_tree[:, None, None, :], jnp.exp(tree_scores - peaks[..., None]), 0.0
        )
        totals = jnp.sum(cache_weights, axis=3) + jnp.sum(tree_weights, axis=3)
        group_sums = jnp.einsum(
            "igqp,pgd->igqd",
            cache_weights.astype(jnp.bfloat16),
            block_values,
            preferred_element_type=jnp.float32,
        )
        group_sums = group_sums + jnp.einsum(
            "igqr,rgd->igqd",
            tree_weights.astype(jnp.bfloat16),
            local_tree_values,
            preferred_element_type=jnp.float32,
        )
        floored = jnp.maximum(totals, 1.0)
        partial_value = group_sums / floored[..., None]
        log_total = peaks + jnp.log(floored)
        return (
            partial_value.reshape(node_count, heads_local, HD),
            log_total.reshape(node_count, heads_local),
        )

    partials, log_totals = lax.map(one_group, jnp.arange(n_hi, dtype=jnp.int32))
    top = jnp.max(log_totals, axis=0)
    weights = jnp.exp(log_totals - top)
    den = jnp.sum(weights, axis=0)
    acc = jnp.sum(weights[..., None] * partials, axis=0)
    payload = jnp.concatenate(
        [acc.reshape(node_count, heads_local * HD), den, top], axis=1
    ).reshape(n_lo, rows_owned, heads_local * HD + 2 * heads_local)
    gathered = lax.all_to_all(payload, "rl", split_axis=0, concat_axis=0, tiled=True)
    got_acc = gathered[:, :, : heads_local * HD].reshape(n_lo, rows_owned, heads_local, HD)
    got_den = gathered[:, :, heads_local * HD : heads_local * HD + heads_local]
    got_top = gathered[:, :, heads_local * HD + heads_local :]
    highest = jnp.max(got_top, axis=0)
    scale = jnp.exp(got_top - highest)
    num = jnp.sum(scale[..., None] * got_acc, axis=0)
    total = jnp.sum(scale * got_den, axis=0)
    merged = (num / total[..., None]).reshape(rows_owned, heads_local * HD)
    row_nodes = quarter * rows_owned + jnp.arange(rows_owned, dtype=jnp.int32)
    live_size = lax.dynamic_index_in_dim(tree_sizes, request, 0, keepdims=False)
    live_rows = row_nodes < live_size
    return jnp.where(live_rows[:, None], merged, 0.0).astype(jnp.bfloat16)


def solution(mesh):

    def run(
        queries, cache_keys, cache_values, tree_keys, tree_values, parents, tree_sizes, cache_lens
    ):
        n_hi = cache_keys.shape[0]
        n_lo = mesh.shape["req"] // n_hi
        split = Mesh(mesh.devices.reshape(n_hi, n_lo, mesh.shape["head"]), ("rh", "rl", "head"))
        rows = ("rh", "rl")
        placed = (
            P(("rh", "rl", "head"), None),
            P(None, rows, "head"),
            P(None, rows, "head"),
            P(rows, "head"),
            P(rows, "head"),
            P(),
            P(),
            P(),
        )
        return jax.shard_map(
            body, mesh=split, in_specs=placed, out_specs=P(rows, "head"), check_vma=False
        )(
            queries,
            cache_keys,
            cache_values,
            tree_keys,
            tree_values,
            parents,
            tree_sizes,
            cache_lens,
        )

    return run
```

profile of v0, /device:TPU:1, one launch (start us, length us, event | category | flops | bytes accessed | tf_op | source)
XLA Modules:
  0.0 273.4 jit_solution(10835699050133776124)
XLA Ops:
  0.0 9.1 %all-to-all-start.1 = ((bf16[4,8,2048]{2,0,1:T(4,128)(2,1)}), bf16[4,8,2048]{2,0,1:T(4,128)(2,1)S(1)}, u32[]{:S(2)}, u32[]{:S(2)}) async-start(bf16[4,8,2048]{2,0,1:T(4,128)(2,1)} %bitcast.168), calls=%async_computation.1 | async-start | bytes 262144 | tf_op jit(solution)/shard_map/all_to_all | solution.py:41
  9.2 2.9 %copy.62 = bf16[8,1024,128]{1,2,0:T(8,128)(2,1)S(1)} copy(bf16[8,1024,128]{2,1,0:T(8,128)(2,1)} %param.12) | data formatting | bytes 4194304 | tf_op args[2]
  12.0 3.9 %copy.61 = bf16[8,1024,128]{1,2,0:T(8,128)(2,1)} copy(bf16[8,1024,128]{2,1,0:T(8,128)(2,1)} %param.11) | data formatting | bytes 4194304 | tf_op args[1]
  16.0 4.2 %pad_maximum_fusion = bf16[8,1024,256]{1,2,0:T(8,128)(2,1)} fusion(bf16[8,1024,128]{1,2,0:T(8,128)(2,1)S(1)} %copy.62, bf16[8,1024,128]{1,2,0:T(8,128)(2,1)} %copy.61), kind=kLoop, calls=%fused_computation.47 | loop fusion | flops 8388608 | bytes 8388608 | tf_op jit(solution)/shard_map/concatenate | solution.py:44
  20.2 6.7 %all-to-all-start = ((bf16[8,1024,256]{1,2,0:T(8,128)(2,1)}), bf16[8,1024,256]{1,2,0:T(8,128)(2,1)}, u32[]{:S(2)}, u32[]{:S(2)}) async-start(bf16[8,1024,256]{1,2,0:T(8,128)(2,1)} %pad_maximum_fusion), calls=%async_computation | async-start | bytes 8388608 | tf_op jit(solution)/shard_map/all_to_all | solution.py:45
  27.5 0.9 fusion.38
  29.7 47.9 %all_gather.3 = bf16[128,2048]{1,0:T(8,128)(2,1)S(1)} all-gather(bf16[32,2048]{1,0:T(8,128)(2,1)S(1)} %all_to_all.28), channel_id=1, replica_groups=mesh['rh'=8,'rl'=4,'head'=8] {'rl'}, dimensions={0}, use_global_device_ids=true | all-gather | bytes 655360 | tf_op jit(solution)/shard_map/all_gather | solution.py:42
  78.5 6.5 %copy.69 = bf16[8,1024,2,1,128]{4,1,3,2,0:T(8,128)(2,1)} copy(bf16[8,1024,2,1,128]{1,4,2,0,3:T(8,128)(2,1)} %bitcast.20) | data formatting | bytes 8388608 | tf_op jit(solution)/shard_map/while | solution.py:104
  85.0 160.4 %while.14 = (s32[]{:T(128)}, f32[8,128,16,128]{1,3,2,0:T(8,128)}, f32[8,128,16]{1,2,0:T(8,128)S(1)}, s32[8]{0:T(128)S(1)}, bf16[8,1024,2,1,128]{4,1,3,2,0:T(8,12...) while((s32[]{:T(128)}, f32[8,128,16,128]{1,3,2,0:T(8,128)}, ...), condition=%wide.region_5.6_spmd, body=%wide.region_0.5_spmd.sunk | while | flops 1119164416 | bytes 55485768 | solution.py:104
  85.0 0.7 dynamic_slice.52
  88.9 5.5 %bitcast_reduce_fusion.2 = (f32[128,16]{0,1:T(8,128)S(1)}, f32[1024,128,16]{1,0,2:T(8,128)}) fusion(pred[1024]{0:T(1024)(128)(4,1)S(1)} %add_compare_fusion.3, bf16[128,1,16,128]{3,0,2,1:T(8,128)(2,1)S(1)} %get-tuple-element.349, bf16[8,1024,2,1,128]{4,1,3,2,0:T(8,128)(2,1)} %get-tuple-element.346, s32[]{:T(128)S(6)} %select_n.118), kind=kOutput, calls=%fused_computation.1.clone.1 | convolution fusion | flops 543160320 | bytes 9184260 | tf_op jit(solution)/shard_map/while/body/eval_jaxpr/igqd,pgd->igqp/dot_general | solution.py:63
  95.2 5.8 %fusion.85 = f32[128,128,16]{1,0,2:T(8,128)S(1)} fusion(f32[1024,128,16]{1,0,2:T(8,128)} %get-tuple-element.304, f32[128,16]{0,1:T(8,128)S(1)} %max.47, pred[1024]{0:T(1024)(128)(4,1)S(1)} %add_compare_fusion.3, bf16[8,1024,2,1,128]{4,1,3,2,0:T(8,128)(2,1)} %get-tuple-element.346, s32[]{:T(128)S(6)} %select_n.118), kind=kOutput, calls=%fused_computation.8.clone.1 | convolution fusion | flops 547356672 | bytes 9709572 | tf_op jit(solution)/shard_map/while/body/eval_jaxpr/igqp,pgd->igqd/dot_general | solution.py:84
  101.0 2.5 fusion.86
  103.7 1.3 bitcast_dynamic-update-slice_fusion.5
  105.0 0.7 dynamic_slice.52
  108.9 5.5 %bitcast_reduce_fusion.2 = (f32[128,16]{0,1:T(8,128)S(1)}, f32[1024,128,16]{1,0,2:T(8,128)}) fusion(pred[1024]{0:T(1024)(128)(4,1)S(1)} %add_compare_fusion.3, bf16[128,1,16,128]{3,0,2,1:T(8,128)(2,1)S(1)} %get-tuple-element.349, bf16[8,1024,2,1,128]{4,1,3,2,0:T(8,128)(2,1)} %get-tuple-element.346, s32[]{:T(128)S(6)} %select_n.118), kind=kOutput, calls=%fused_computation.1.clone.1 | convolution fusion | flops 543160320 | bytes 9184260 | tf_op jit(solution)/shard_map/while/body/eval_jaxpr/igqd,pgd->igqp/dot_general | solution.py:63
  115.2 5.8 %fusion.85 = f32[128,128,16]{1,0,2:T(8,128)S(1)} fusion(f32[1024,128,16]{1,0,2:T(8,128)} %get-tuple-element.304, f32[128,16]{0,1:T(8,128)S(1)} %max.47, pred[1024]{0:T(1024)(128)(4,1)S(1)} %add_compare_fusion.3, bf16[8,1024,2,1,128]{4,1,3,2,0:T(8,128)(2,1)} %get-tuple-element.346, s32[]{:T(128)S(6)} %select_n.118), kind=kOutput, calls=%fused_computation.8.clone.1 | convolution fusion | flops 547356672 | bytes 9709572 | tf_op jit(solution)/shard_map/while/body/eval_jaxpr/igqp,pgd->igqd/dot_general | solution.py:84
  121.1 2.5 fusion.86
  123.7 1.4 bitcast_dynamic-update-slice_fusion.5
  129.0 5.5 %bitcast_reduce_fusion.2 = (f32[128,16]{0,1:T(8,128)S(1)}, f32[1024,128,16]{1,0,2:T(8,128)}) fusion(pred[1024]{0:T(1024)(128)(4,1)S(1)} %add_compare_fusion.3, bf16[128,1,16,128]{3,0,2,1:T(8,128)(2,1)S(1)} %get-tuple-element.349, bf16[8,1024,2,1,128]{4,1,3,2,0:T(8,128)(2,1)} %get-tuple-element.346, s32[]{:T(128)S(6)} %select_n.118), kind=kOutput, calls=%fused_computation.1.clone.1 | convolution fusion | flops 543160320 | bytes 9184260 | tf_op jit(solution)/shard_map/while/body/eval_jaxpr/igqd,pgd->igqp/dot_general | solution.py:63
  135.3 5.8 %fusion.85 = f32[128,128,16]{1,0,2:T(8,128)S(1)} fusion(f32[1024,128,16]{1,0,2:T(8,128)} %get-tuple-element.304, f32[128,16]{0,1:T(8,128)S(1)} %max.47, pred[1024]{0:T(1024)(128)(4,1)S(1)} %add_compare_fusion.3, bf16[8,1024,2,1,128]{4,1,3,2,0:T(8,128)(2,1)} %get-tuple-element.346, s32[]{:T(128)S(6)} %select_n.118), kind=kOutput, calls=%fused_computation.8.clone.1 | convolution fusion | flops 547356672 | bytes 9709572 | tf_op jit(solution)/shard_map/while/body/eval_jaxpr/igqp,pgd->igqd/dot_general | solution.py:84
  141.2 2.5 fusion.86
  143.8 1.3 bitcast_dynamic-update-slice_fusion.5
  149.1 5.5 %bitcast_reduce_fusion.2 = (f32[128,16]{0,1:T(8,128)S(1)}, f32[1024,128,16]{1,0,2:T(8,128)}) fusion(pred[1024]{0:T(1024)(128)(4,1)S(1)} %add_compare_fusion.3, bf16[128,1,16,128]{3,0,2,1:T(8,128)(2,1)S(1)} %get-tuple-element.349, bf16[8,1024,2,1,128]{4,1,3,2,0:T(8,128)(2,1)} %get-tuple-element.346, s32[]{:T(128)S(6)} %select_n.118), kind=kOutput, calls=%fused_computation.1.clone.1 | convolution fusion | flops 543160320 | bytes 9184260 | tf_op jit(solution)/shard_map/while/body/eval_jaxpr/igqd,pgd->igqp/dot_general | solution.py:63
  155.3 5.8 %fusion.85 = f32[128,128,16]{1,0,2:T(8,128)S(1)} fusion(f32[1024,128,16]{1,0,2:T(8,128)} %get-tuple-element.304, f32[128,16]{0,1:T(8,128)S(1)} %max.47, pred[1024]{0:T(1024)(128)(4,1)S(1)} %add_compare_fusion.3, bf16[8,1024,2,1,128]{4,1,3,2,0:T(8,128)(2,1)} %get-tuple-element.346, s32[]{:T(128)S(6)} %select_n.118), kind=kOutput, calls=%fused_computation.8.clone.1 | convolution fusion | flops 547356672 | bytes 9709572 | tf_op jit(solution)/shard_map/while/body/eval_jaxpr/igqp,pgd->igqd/dot_general | solution.py:84
  161.2 2.5 fusion.86
  163.8 1.3 bitcast_dynamic-update-slice_fusion.5
  169.1 5.5 %bitcast_reduce_fusion.2 = (f32[128,16]{0,1:T(8,128)S(1)}, f32[1024,128,16]{1,0,2:T(8,128)}) fusion(pred[1024]{0:T(1024)(128)(4,1)S(1)} %add_compare_fusion.3, bf16[128,1,16,128]{3,0,2,1:T(8,128)(2,1)S(1)} %get-tuple-element.349, bf16[8,1024,2,1,128]{4,1,3,2,0:T(8,128)(2,1)} %get-tuple-element.346, s32[]{:T(128)S(6)} %select_n.118), kind=kOutput, calls=%fused_computation.1.clone.1 | convolution fusion | flops 543160320 | bytes 9184260 | tf_op jit(solution)/shard_map/while/body/eval_jaxpr/igqd,pgd->igqp/dot_general | solution.py:63
  175.4 5.8 %fusion.85 = f32[128,128,16]{1,0,2:T(8,128)S(1)} fusion(f32[1024,128,16]{1,0,2:T(8,128)} %get-tuple-element.304, f32[128,16]{0,1:T(8,128)S(1)} %max.47, pred[1024]{0:T(1024)(128)(4,1)S(1)} %add_compare_fusion.3, bf16[8,1024,2,1,128]{4,1,3,2,0:T(8,128)(2,1)} %get-tuple-element.346, s32[]{:T(128)S(6)} %select_n.118), kind=kOutput, calls=%fused_computation.8.clone.1 | convolution fusion | flops 547356672 | bytes 9709572 | tf_op jit(solution)/shard_map/while/body/eval_jaxpr/igqp,pgd->igqd/dot_general | solution.py:84
  181.2 2.5 fusion.86
  183.9 1.3 bitcast_dynamic-update-slice_fusion.5
  189.1 5.5 %bitcast_reduce_fusion.2 = (f32[128,16]{0,1:T(8,128)S(1)}, f32[1024,128,16]{1,0,2:T(8,128)}) fusion(pred[1024]{0:T(1024)(128)(4,1)S(1)} %add_compare_fusion.3, bf16[128,1,16,128]{3,0,2,1:T(8,128)(2,1)S(1)} %get-tuple-element.349, bf16[8,1024,2,1,128]{4,1,3,2,0:T(8,128)(2,1)} %get-tuple-element.346, s32[]{:T(128)S(6)} %select_n.118), kind=kOutput, calls=%fused_computation.1.clone.1 | convolution fusion | flops 543160320 | bytes 9184260 | tf_op jit(solution)/shard_map/while/body/eval_jaxpr/igqd,pgd->igqp/dot_general | solution.py:63
  195.4 5.8 %fusion.85 = f32[128,128,16]{1,0,2:T(8,128)S(1)} fusion(f32[1024,128,16]{1,0,2:T(8,128)} %get-tuple-element.304, f32[128,16]{0,1:T(8,128)S(1)} %max.47, pred[1024]{0:T(1024)(128)(4,1)S(1)} %add_compare_fusion.3, bf16[8,1024,2,1,128]{4,1,3,2,0:T(8,128)(2,1)} %get-tuple-element.346, s32[]{:T(128)S(6)} %select_n.118), kind=kOutput, calls=%fused_computation.8.clone.1 | convolution fusion | flops 547356672 | bytes 9709572 | tf_op jit(solution)/shard_map/while/body/eval_jaxpr/igqp,pgd->igqd/dot_general | solution.py:84
  201.3 2.5 fusion.86
  203.9 1.4 bitcast_dynamic-update-slice_fusion.5
  209.2 5.5 %bitcast_reduce_fusion.2 = (f32[128,16]{0,1:T(8,128)S(1)}, f32[1024,128,16]{1,0,2:T(8,128)}) fusion(pred[1024]{0:T(1024)(128)(4,1)S(1)} %add_compare_fusion.3, bf16[128,1,16,128]{3,0,2,1:T(8,128)(2,1)S(1)} %get-tuple-element.349, bf16[8,1024,2,1,128]{4,1,3,2,0:T(8,128)(2,1)} %get-tuple-element.346, s32[]{:T(128)S(6)} %select_n.118), kind=kOutput, calls=%fused_computation.1.clone.1 | convolution fusion | flops 543160320 | bytes 9184260 | tf_op jit(solution)/shard_map/while/body/eval_jaxpr/igqd,pgd->igqp/dot_general | solution.py:63
  215.5 5.8 %fusion.85 = f32[128,128,16]{1,0,2:T(8,128)S(1)} fusion(f32[1024,128,16]{1,0,2:T(8,128)} %get-tuple-element.304, f32[128,16]{0,1:T(8,128)S(1)} %max.47, pred[1024]{0:T(1024)(128)(4,1)S(1)} %add_compare_fusion.3, bf16[8,1024,2,1,128]{4,1,3,2,0:T(8,128)(2,1)} %get-tuple-element.346, s32[]{:T(128)S(6)} %select_n.118), kind=kOutput, calls=%fused_computation.8.clone.1 | convolution fusion | flops 547356672 | bytes 9709572 | tf_op jit(solution)/shard_map/while/body/eval_jaxpr/igqp,pgd->igqd/dot_general | solution.py:84
  221.3 2.5 fusion.86
  224.0 1.4 bitcast_dynamic-update-slice_fusion.5
  229.3 5.5 %bitcast_reduce_fusion.2 = (f32[128,16]{0,1:T(8,128)S(1)}, f32[1024,128,16]{1,0,2:T(8,128)}) fusion(pred[1024]{0:T(1024)(128)(4,1)S(1)} %add_compare_fusion.3, bf16[128,1,16,128]{3,0,2,1:T(8,128)(2,1)S(1)} %get-tuple-element.349, bf16[8,1024,2,1,128]{4,1,3,2,0:T(8,128)(2,1)} %get-tuple-element.346, s32[]{:T(128)S(6)} %select_n.118), kind=kOutput, calls=%fused_computation.1.clone.1 | convolution fusion | flops 543160320 | bytes 9184260 | tf_op jit(solution)/shard_map/while/body/eval_jaxpr/igqd,pgd->igqp/dot_general | solution.py:63
  235.5 5.8 %fusion.85 = f32[128,128,16]{1,0,2:T(8,128)S(1)} fusion(f32[1024,128,16]{1,0,2:T(8,128)} %get-tuple-element.304, f32[128,16]{0,1:T(8,128)S(1)} %max.47, pred[1024]{0:T(1024)(128)(4,1)S(1)} %add_compare_fusion.3, bf16[8,1024,2,1,128]{4,1,3,2,0:T(8,128)(2,1)} %get-tuple-element.346, s32[]{:T(128)S(6)} %select_n.118), kind=kOutput, calls=%fused_computation.8.clone.1 | convolution fusion | flops 547356672 | bytes 9709572 | tf_op jit(solution)/shard_map/while/body/eval_jaxpr/igqp,pgd->igqd/dot_general | solution.py:84
  241.4 2.5 fusion.86
  244.0 1.3 bitcast_dynamic-update-slice_fusion.5
  245.5 4.8 %multiply_reduce_fusion = f32[128,16,128]{0,2,1:T(8,128)S(1)} fusion(f32[8,128,16,128]{1,3,2,0:T(8,128)} %get-tuple-element.146, f32[8,128,16]{1,2,0:T(8,128)S(1)} %get-tuple-element.224), kind=kLoop, calls=%fused_computation.46 | loop fusion | flops 3932160 | bytes 9502720 | tf_op jit(solution)/shard_map/reduce_sum | solution.py:108
  251.1 1.2 concatenate.17
  252.2 5.2 %all-to-all-start.2 = ((f32[4,32,2080]{2,1,0:T(8,128)}), f32[4,32,2080]{2,1,0:T(8,128)S(1)}, u32[]{:S(2)}, u32[]{:S(2)}) async-start(f32[4,32,2080]{2,1,0:T(8,128)} %concatenate.17), calls=%async_computation.2 | async-start | bytes 2228224 | tf_op jit(solution)/shard_map/all_to_all | solution.py:112
  258.7 13.1 %all-to-all-done.2 = f32[4,32,2080]{2,1,0:T(8,128)S(1)} async-done(((f32[4,32,2080]{2,1,0:T(8,128)}), f32[4,32,2080]{2,1,0:T(8,128)S(1)}, u32[]{:S(2)}, u32[]{:S(2)}) %all-to-all-start.2) | async-done | bytes 1064992 | tf_op jit(solution)/shard_map/all_to_all | solution.py:112
  272.6 0.8 fusion.48
  (134 shorter events, 16.0 us)
Async XLA Ops:
  0.0 78.3 %copy-start = (bf16[32,128]{1,0:T(8,128)(2,1)S(1)}, bf16[32,128]{1,0:T(8,128)(2,1)}, u32[]{:S(2)}) copy-start(bf16[32,128]{1,0:T(8,128)(2,1)} %param.13) | copy-start | bytes 24580
  0.0 20.2 %all-to-all-start.1 = ((bf16[4,8,2048]{2,0,1:T(4,128)(2,1)}), bf16[4,8,2048]{2,0,1:T(4,128)(2,1)S(1)}, u32[]{:S(2)}, u32[]{:S(2)}) async-start(bf16[4,8,2048]{2,0,1:T(4,128)(2,1)} %bitcast.168), calls=%async_computation.1 | async-start | bytes 262144 | tf_op jit(solution)/shard_map/all_to_all | solution.py:41
  16.0 10.9 %copy-start.3 = (s32[8]{0:T(128)S(1)}, s32[8]{0:T(128)}, u32[]{:S(2)}) copy-start(s32[8]{0:T(128)} %param.17) | copy-start | bytes 100
  16.0 11.5 %copy-start.2 = (s32[8,128]{1,0:T(8,128)S(1)}, s32[8,128]{1,0:T(8,128)}, u32[]{:S(2)}) copy-start(s32[8,128]{1,0:T(8,128)} %param.15) | copy-start | bytes 12292
  20.2 58.3 %all-to-all-start = ((bf16[8,1024,256]{1,2,0:T(8,128)(2,1)}), bf16[8,1024,256]{1,2,0:T(8,128)(2,1)}, u32[]{:S(2)}, u32[]{:S(2)}) async-start(bf16[8,1024,256]{1,2,0:T(8,128)(2,1)} %pad_maximum_fusion), calls=%async_computation | async-start | bytes 8388608 | tf_op jit(solution)/shard_map/all_to_all | solution.py:45
  26.8 58.1 %copy-start.1 = (bf16[32,128]{1,0:T(8,128)(2,1)S(1)}, bf16[32,128]{1,0:T(8,128)(2,1)}, u32[]{:S(2)}) copy-start(bf16[32,128]{1,0:T(8,128)(2,1)} %param.14) | copy-start | bytes 24580
  95.1 5.9 %slice-start = ((s8[8388608]{0:T(1024)(128)(4,1)}), s8[4194304]{0:T(1024)(128)(4,1)S(1)}, s32[]{:S(2)}) async-start(s8[8388608]{0:T(1024)(128)(4,1)} %bitcast.160), calls=%async_computation.3 | async-start | bytes 8388608 | tf_op jit(solution)/shard_map/while
  95.2 5.9 %slice-start.1 = ((s8[8388608]{0:T(1024)(128)(4,1)}), s8[4194304]{0:T(1024)(128)(4,1)S(1)}, s32[]{:S(2)}) async-start(s8[8388608]{0:T(1024)(128)(4,1)} %bitcast.160), calls=%async_computation.4 | async-start | bytes 8388608 | tf_op jit(solution)/shard_map/while
  115.1 5.9 %slice-start = ((s8[8388608]{0:T(1024)(128)(4,1)}), s8[4194304]{0:T(1024)(128)(4,1)S(1)}, s32[]{:S(2)}) async-start(s8[8388608]{0:T(1024)(128)(4,1)} %bitcast.160), calls=%async_computation.3 | async-start | bytes 8388608 | tf_op jit(solution)/shard_map/while
  115.2 5.9 %slice-start.1 = ((s8[8388608]{0:T(1024)(128)(4,1)}), s8[4194304]{0:T(1024)(128)(4,1)S(1)}, s32[]{:S(2)}) async-start(s8[8388608]{0:T(1024)(128)(4,1)} %bitcast.160), calls=%async_computation.4 | async-start | bytes 8388608 | tf_op jit(solution)/shard_map/while
  135.2 5.9 %slice-start = ((s8[8388608]{0:T(1024)(128)(4,1)}), s8[4194304]{0:T(1024)(128)(4,1)S(1)}, s32[]{:S(2)}) async-start(s8[8388608]{0:T(1024)(128)(4,1)} %bitcast.160), calls=%async_computation.3 | async-start | bytes 8388608 | tf_op jit(solution)/shard_map/while
  135.3 5.9 %slice-start.1 = ((s8[8388608]{0:T(1024)(128)(4,1)}), s8[4194304]{0:T(1024)(128)(4,1)S(1)}, s32[]{:S(2)}) async-start(s8[8388608]{0:T(1024)(128)(4,1)} %bitcast.160), calls=%async_computation.4 | async-start | bytes 8388608 | tf_op jit(solution)/shard_map/while
  155.2 5.9 %slice-start = ((s8[8388608]{0:T(1024)(128)(4,1)}), s8[4194304]{0:T(1024)(128)(4,1)S(1)}, s32[]{:S(2)}) async-start(s8[8388608]{0:T(1024)(128)(4,1)} %bitcast.160), calls=%async_computation.3 | async-start | bytes 8388608 | tf_op jit(solution)/shard_map/while
  155.3 5.9 %slice-start.1 = ((s8[8388608]{0:T(1024)(128)(4,1)}), s8[4194304]{0:T(1024)(128)(4,1)S(1)}, s32[]{:S(2)}) async-start(s8[8388608]{0:T(1024)(128)(4,1)} %bitcast.160), calls=%async_computation.4 | async-start | bytes 8388608 | tf_op jit(solution)/shard_map/while
  175.3 5.9 %slice-start = ((s8[8388608]{0:T(1024)(128)(4,1)}), s8[4194304]{0:T(1024)(128)(4,1)S(1)}, s32[]{:S(2)}) async-start(s8[8388608]{0:T(1024)(128)(4,1)} %bitcast.160), calls=%async_computation.3 | async-start | bytes 8388608 | tf_op jit(solution)/shard_map/while
  175.4 5.9 %slice-start.1 = ((s8[8388608]{0:T(1024)(128)(4,1)}), s8[4194304]{0:T(1024)(128)(4,1)S(1)}, s32[]{:S(2)}) async-start(s8[8388608]{0:T(1024)(128)(4,1)} %bitcast.160), calls=%async_computation.4 | async-start | bytes 8388608 | tf_op jit(solution)/shard_map/while
  195.3 5.9 %slice-start = ((s8[8388608]{0:T(1024)(128)(4,1)}), s8[4194304]{0:T(1024)(128)(4,1)S(1)}, s32[]{:S(2)}) async-start(s8[8388608]{0:T(1024)(128)(4,1)} %bitcast.160), calls=%async_computation.3 | async-start | bytes 8388608 | tf_op jit(solution)/shard_map/while
  195.4 5.9 %slice-start.1 = ((s8[8388608]{0:T(1024)(128)(4,1)}), s8[4194304]{0:T(1024)(128)(4,1)S(1)}, s32[]{:S(2)}) async-start(s8[8388608]{0:T(1024)(128)(4,1)} %bitcast.160), calls=%async_computation.4 | async-start | bytes 8388608 | tf_op jit(solution)/shard_map/while
  215.4 5.9 %slice-start = ((s8[8388608]{0:T(1024)(128)(4,1)}), s8[4194304]{0:T(1024)(128)(4,1)S(1)}, s32[]{:S(2)}) async-start(s8[8388608]{0:T(1024)(128)(4,1)} %bitcast.160), calls=%async_computation.3 | async-start | bytes 8388608 | tf_op jit(solution)/shard_map/while
  215.5 5.9 %slice-start.1 = ((s8[8388608]{0:T(1024)(128)(4,1)}), s8[4194304]{0:T(1024)(128)(4,1)S(1)}, s32[]{:S(2)}) async-start(s8[8388608]{0:T(1024)(128)(4,1)} %bitcast.160), calls=%async_computation.4 | async-start | bytes 8388608 | tf_op jit(solution)/shard_map/while
  235.4 5.9 %slice-start = ((s8[8388608]{0:T(1024)(128)(4,1)}), s8[4194304]{0:T(1024)(128)(4,1)S(1)}, s32[]{:S(2)}) async-start(s8[8388608]{0:T(1024)(128)(4,1)} %bitcast.160), calls=%async_computation.3 | async-start | bytes 8388608 | tf_op jit(solution)/shard_map/while
  235.5 5.9 %slice-start.1 = ((s8[8388608]{0:T(1024)(128)(4,1)}), s8[4194304]{0:T(1024)(128)(4,1)S(1)}, s32[]{:S(2)}) async-start(s8[8388608]{0:T(1024)(128)(4,1)} %bitcast.160), calls=%async_computation.4 | async-start | bytes 8388608 | tf_op jit(solution)/shard_map/while
  245.5 11.9 %copy-start.4 = (s32[8]{0:T(128)S(1)}, s32[8]{0:T(128)}, u32[]{:S(2)}) copy-start(s32[8]{0:T(128)} %param.16) | copy-start | bytes 100
  252.2 19.5 %all-to-all-start.2 = ((f32[4,32,2080]{2,1,0:T(8,128)}), f32[4,32,2080]{2,1,0:T(8,128)S(1)}, u32[]{:S(2)}, u32[]{:S(2)}) async-start(f32[4,32,2080]{2,1,0:T(8,128)} %concatenate.17), calls=%async_computation.2 | async-start | bytes 2228224 | tf_op jit(solution)/shard_map/all_to_all | solution.py:112
where the time goes:
time: 275 us; the launch traced here: 273 us
  matrix products  103 us (37%)
  blocking collectives  47.9 us (17%)
  other arithmetic  36.8 us (13%)
  loops' own time  27.8 us (10%)
  local copies, waits for them, and re-layouts  23.5 us (9%)
  starting transfers between devices  21 us (8%)
  waiting for transfers between devices  13.1 us (5%)
    all_gather x1, blocking collectives, body(): query_block = lax.all_gather(by_head, 'rl', axis=0, tiled=True)  47.9 us
    dot_general x8, matrix products, one_group(): jnp.einsum('igqp,pgd->igqd', cache_weights.astype(jnp.bfloat16), block_va...  46.3 us
    dot_general x8, matrix products, one_group(): jnp.einsum('igqd,pgd->igqp', query_block, block_keys, preferred_element_t...  43.9 us
    another operation x1, loops' own time, body(): partials, log_totals = lax.map(one_group, jnp.arange(n_hi, dtype=jnp.int32))  27.8 us
    reduce_sum x16, other arithmetic, one_group(): totals = jnp.sum(cache_weights, axis=3) + jnp.sum(tree_weights, axis=3)  20.8 us
    all_to_all x1, waiting for transfers between devices, body(): lax.all_to_all(payload, 'rl', split_axis=0, concat_axis=0, tiled=True)  13.1 us
    dot_general x8, matrix products, one_group(): jnp.einsum('igqr,rgd->igqd', tree_weights.astype(jnp.bfloat16), local_tre...  10.8 us
    all_to_all x1, starting transfers between devices, body(): lax.all_to_all(queries, 'head', split_axis=1, concat_axis=0, tiled=True)  9.15 us
  transfers between devices with their start and end apart: 3, of which 1 were waited for; matrix products, arithmetic and copies ran while one was open for 6% of the time, Pallas kernels for 0%

commit v1 on v0

--- a/solution.py
+++ b/solution.py
@@ -38,7 +38,16 @@
     heads_local = kv_local * group_size
     node_count = parents.shape[1]
     rows_owned = tree_keys.shape[0]
-    by_head = lax.all_to_all(queries, "head", split_axis=1, concat_axis=0, tiled=True)
+
+    def point_fill(panel, dimension_no, join_dim):
+        x_new = jax.lax.axis_size("head")
+        v_now = jnp.split(panel, x_new, dimension_no)
+        new = jnp.stack(v_now, axis=0)
+        main = jax.lax.all_to_all(new, "head", 0, 0)
+        then = jnp.concatenate(main, axis=join_dim)
+        return then
+
+    by_head = point_fill(queries, 1, 0)
     query_block = lax.all_gather(by_head, "rl", axis=0, tiled=True)
     query_block = query_block.reshape(node_count, kv_local, group_size, HD)
     both = jnp.concatenate([cache_keys, cache_values], axis=2)

time: 275 us -> 286 us (1.040)
  local copies, waits for them, and re-layouts: 23.5 us -> 34.1 us
    unnamed x12 -> x19, local copies, waits for them, and re-layouts: 6.81 us -> 16.1 us
where the time goes in v1:
time: 286 us; the launch traced here: 284 us
  matrix products  103 us (36%)
  blocking collectives  47.9 us (17%)
  other arithmetic  36.8 us (13%)
  local copies, waits for them, and re-layouts  34.1 us (12%)
  loops' own time  27.8 us (10%)
  starting transfers between devices  20.8 us (7%)
  waiting for transfers between devices  13.1 us (5%)
    all_gather x1, blocking collectives, body(): query_block = lax.all_gather(by_head, 'rl', axis=0, tiled=True)  47.9 us
    dot_general x8, matrix products, one_group(): jnp.einsum('igqp,pgd->igqd', cache_weights.astype(jnp.bfloat16), block_va...  46.3 us
    dot_general x8, matrix products, one_group(): jnp.einsum('igqd,pgd->igqp', query_block, block_keys, preferred_element_t...  43.9 us
    another operation x1, loops' own time, body(): partials, log_totals = lax.map(one_group, jnp.arange(n_hi, dtype=jnp.int32))  27.8 us
    reduce_sum x16, other arithmetic, one_group(): totals = jnp.sum(cache_weights, axis=3) + jnp.sum(tree_weights, axis=3)  20.8 us
    unnamed x19, local copies, waits for them, and re-layouts  16.1 us
    all_to_all x1, waiting for transfers between devices, body(): lax.all_to_all(payload, 'rl', split_axis=0, concat_axis=0, tiled=True)  13.1 us
    dot_general x8, matrix products, one_group(): jnp.einsum('igqr,rgd->igqd', tree_weights.astype(jnp.bfloat16), local_tre...  10.8 us
  transfers between devices with their start and end apart: 3, of which 1 were waited for; matrix products, arithmetic and copies ran while one was open for 6% of the time, Pallas kernels for 0%

profile of v1, /device:TPU:1, one launch (start us, length us, event | category | flops | bytes accessed | tf_op | source)
XLA Modules:
  0.0 283.9 jit_solution(181621779907443237)
XLA Ops:
  0.0 1.3 constant_dynamic-update-slice_fusion.7
  1.3 1.3 constant_dynamic-update-slice_fusion.6
  2.7 1.3 constant_dynamic-update-slice_fusion.5
  4.0 1.3 constant_dynamic-update-slice_fusion.4
  5.3 1.3 constant_dynamic-update-slice_fusion.3
  6.7 1.3 constant_dynamic-update-slice_fusion.2
  8.0 1.3 constant_dynamic-update-slice_fusion.1
  10.6 9.0 %all-to-all-start.1 = ((bf16[8,4,2048]{2,1,0:T(4,128)(2,1)}), bf16[8,4,2048]{2,1,0:T(4,128)(2,1)S(1)}, u32[]{:S(2)}, u32[]{:S(2)}) async-start(bf16[8,4,2048]{2,1,0:T(4,128)(2,1)} %constant_dynamic-update-slice_fusion), calls=%async_computation.1 | async-start | bytes 262144 | tf_op jit(solution)/shard_map/all_to_all | solution.py:46
  19.7 2.9 %copy.72 = bf16[8,1024,128]{1,2,0:T(8,128)(2,1)S(1)} copy(bf16[8,1024,128]{2,1,0:T(8,128)(2,1)} %param.12) | data formatting | bytes 4194304 | tf_op args[2]
  22.5 3.9 %copy.71 = bf16[8,1024,128]{1,2,0:T(8,128)(2,1)} copy(bf16[8,1024,128]{2,1,0:T(8,128)(2,1)} %param.11) | data formatting | bytes 4194304 | tf_op args[1]
  26.5 4.2 %pad_maximum_fusion = bf16[8,1024,256]{1,2,0:T(8,128)(2,1)} fusion(bf16[8,1024,128]{1,2,0:T(8,128)(2,1)S(1)} %copy.72, bf16[8,1024,128]{1,2,0:T(8,128)(2,1)} %copy.71), kind=kLoop, calls=%fused_computation.47 | loop fusion | flops 8388608 | bytes 8388608 | tf_op jit(solution)/shard_map/concatenate | solution.py:53
  30.7 6.7 %all-to-all-start = ((bf16[8,1024,256]{1,2,0:T(8,128)(2,1)}), bf16[8,1024,256]{1,2,0:T(8,128)(2,1)}, u32[]{:S(2)}, u32[]{:S(2)}) async-start(bf16[8,1024,256]{1,2,0:T(8,128)(2,1)} %pad_maximum_fusion), calls=%async_computation | async-start | bytes 8388608 | tf_op jit(solution)/shard_map/all_to_all | solution.py:54
  40.3 47.9 %all_gather.3 = bf16[128,2048]{1,0:T(8,128)(2,1)S(1)} all-gather(bf16[32,2048]{1,0:T(8,128)(2,1)S(1)} %reshape.223), channel_id=1, replica_groups=mesh['rh'=8,'rl'=4,'head'=8] {'rl'}, dimensions={0}, use_global_device_ids=true | all-gather | bytes 655360 | tf_op jit(solution)/shard_map/all_gather | solution.py:51
  89.0 6.5 %copy.78 = bf16[8,1024,2,1,128]{4,1,3,2,0:T(8,128)(2,1)} copy(bf16[8,1024,2,1,128]{1,4,2,0,3:T(8,128)(2,1)} %bitcast.20) | data formatting | bytes 8388608 | tf_op jit(solution)/shard_map/while | solution.py:113
  95.5 160.4 %while.14 = (s32[]{:T(128)}, f32[8,128,16,128]{1,3,2,0:T(8,128)}, f32[8,128,16]{1,2,0:T(8,128)S(1)}, s32[8]{0:T(128)S(1)}, bf16[8,1024,2,1,128]{4,1,3,2,0:T(8,12...) while((s32[]{:T(128)}, f32[8,128,16,128]{1,3,2,0:T(8,128)}, ...), condition=%wide.region_5.6_spmd, body=%wide.region_0.5_spmd.sunk | while | flops 1119164416 | bytes 55485768 | solution.py:113
  99.4 5.5 %bitcast_reduce_fusion.2 = (f32[128,16]{0,1:T(8,128)S(1)}, f32[1024,128,16]{1,0,2:T(8,128)}) fusion(pred[1024]{0:T(1024)(128)(4,1)S(1)} %add_compare_fusion.3, bf16[128,1,16,128]{3,0,2,1:T(8,128)(2,1)S(1)} %get-tuple-element.361, bf16[8,1024,2,1,128]{4,1,3,2,0:T(8,128)(2,1)} %get-tuple-element.358, s32[]{:T(128)S(6)} %select_n.118), kind=kOutput, calls=%fused_computation.1.clone.1 | convolution fusion | flops 543160320 | bytes 9184260 | tf_op jit(solution)/shard_map/while/body/eval_jaxpr/igqd,pgd->igqp/dot_general | solution.py:72
  105.7 5.8 %fusion.84 = f32[128,128,16]{1,0,2:T(8,128)S(1)} fusion(f32[1024,128,16]{1,0,2:T(8,128)} %get-tuple-element.316, f32[128,16]{0,1:T(8,128)S(1)} %max.47, pred[1024]{0:T(1024)(128)(4,1)S(1)} %add_compare_fusion.3, bf16[8,1024,2,1,128]{4,1,3,2,0:T(8,128)(2,1)} %get-tuple-element.358, s32[]{:T(128)S(6)} %select_n.118), kind=kOutput, calls=%fused_computation.8.clone.1 | convolution fusion | flops 547356672 | bytes 9709572 | tf_op jit(solution)/shard_map/while/body/eval_jaxpr/igqp,pgd->igqd/dot_general | solution.py:93
  111.5 2.5 fusion.85
  114.2 1.3 bitcast_dynamic-update-slice_fusion.5
  119.4 5.5 %bitcast_reduce_fusion.2 = (f32[128,16]{0,1:T(8,128)S(1)}, f32[1024,128,16]{1,0,2:T(8,128)}) fusion(pred[1024]{0:T(1024)(128)(4,1)S(1)} %add_compare_fusion.3, bf16[128,1,16,128]{3,0,2,1:T(8,128)(2,1)S(1)} %get-tuple-element.361, bf16[8,1024,2,1,128]{4,1,3,2,0:T(8,128)(2,1)} %get-tuple-element.358, s32[]{:T(128)S(6)} %select_n.118), kind=kOutput, calls=%fused_computation.1.clone.1 | convolution fusion | flops 543160320 | bytes 9184260 | tf_op jit(solution)/shard_map/while/body/eval_jaxpr/igqd,pgd->igqp/dot_general | solution.py:72
  125.7 5.8 %fusion.84 = f32[128,128,16]{1,0,2:T(8,128)S(1)} fusion(f32[1024,128,16]{1,0,2:T(8,128)} %get-tuple-element.316, f32[128,16]{0,1:T(8,128)S(1)} %max.47, pred[1024]{0:T(1024)(128)(4,1)S(1)} %add_compare_fusion.3, bf16[8,1024,2,1,128]{4,1,3,2,0:T(8,128)(2,1)} %get-tuple-element.358, s32[]{:T(128)S(6)} %select_n.118), kind=kOutput, calls=%fused_computation.8.clone.1 | convolution fusion | flops 547356672 | bytes 9709572 | tf_op jit(solution)/shard_map/while/body/eval_jaxpr/igqp,pgd->igqd/dot_general | solution.py:93
  131.6 2.5 fusion.85
  134.2 1.4 bitcast_dynamic-update-slice_fusion.5
  139.5 5.5 %bitcast_reduce_fusion.2 = (f32[128,16]{0,1:T(8,128)S(1)}, f32[1024,128,16]{1,0,2:T(8,128)}) fusion(pred[1024]{0:T(1024)(128)(4,1)S(1)} %add_compare_fusion.3, bf16[128,1,16,128]{3,0,2,1:T(8,128)(2,1)S(1)} %get-tuple-element.361, bf16[8,1024,2,1,128]{4,1,3,2,0:T(8,128)(2,1)} %get-tuple-element.358, s32[]{:T(128)S(6)} %select_n.118), kind=kOutput, calls=%fused_computation.1.clone.1 | convolution fusion | flops 543160320 | bytes 9184260 | tf_op jit(solution)/shard_map/while/body/eval_jaxpr/igqd,pgd->igqp/dot_general | solution.py:72
  145.8 5.8 %fusion.84 = f32[128,128,16]{1,0,2:T(8,128)S(1)} fusion(f32[1024,128,16]{1,0,2:T(8,128)} %get-tuple-element.316, f32[128,16]{0,1:T(8,128)S(1)} %max.47, pred[1024]{0:T(1024)(128)(4,1)S(1)} %add_compare_fusion.3, bf16[8,1024,2,1,128]{4,1,3,2,0:T(8,128)(2,1)} %get-tuple-element.358, s32[]{:T(128)S(6)} %select_n.118), kind=kOutput, calls=%fused_computation.8.clone.1 | convolution fusion | flops 547356672 | bytes 9709572 | tf_op jit(solution)/shard_map/while/body/eval_jaxpr/igqp,pgd->igqd/dot_general | solution.py:93
  151.6 2.5 fusion.85
  154.3 1.3 bitcast_dynamic-update-slice_fusion.5
  159.6 5.5 %bitcast_reduce_fusion.2 = (f32[128,16]{0,1:T(8,128)S(1)}, f32[1024,128,16]{1,0,2:T(8,128)}) fusion(pred[1024]{0:T(1024)(128)(4,1)S(1)} %add_compare_fusion.3, bf16[128,1,16,128]{3,0,2,1:T(8,128)(2,1)S(1)} %get-tuple-element.361, bf16[8,1024,2,1,128]{4,1,3,2,0:T(8,128)(2,1)} %get-tuple-element.358, s32[]{:T(128)S(6)} %select_n.118), kind=kOutput, calls=%fused_computation.1.clone.1 | convolution fusion | flops 543160320 | bytes 9184260 | tf_op jit(solution)/shard_map/while/body/eval_jaxpr/igqd,pgd->igqp/dot_general | solution.py:72
  165.8 5.8 %fusion.84 = f32[128,128,16]{1,0,2:T(8,128)S(1)} fusion(f32[1024,128,16]{1,0,2:T(8,128)} %get-tuple-element.316, f32[128,16]{0,1:T(8,128)S(1)} %max.47, pred[1024]{0:T(1024)(128)(4,1)S(1)} %add_compare_fusion.3, bf16[8,1024,2,1,128]{4,1,3,2,0:T(8,128)(2,1)} %get-tuple-element.358, s32[]{:T(128)S(6)} %select_n.118), kind=kOutput, calls=%fused_computation.8.clone.1 | convolution fusion | flops 547356672 | bytes 9709572 | tf_op jit(solution)/shard_map/while/body/eval_jaxpr/igqp,pgd->igqd/dot_general | solution.py:93
  171.7 2.5 fusion.85
  174.3 1.3 bitcast_dynamic-update-slice_fusion.5
  179.6 5.5 %bitcast_reduce_fusion.2 = (f32[128,16]{0,1:T(8,128)S(1)}, f32[1024,128,16]{1,0,2:T(8,128)}) fusion(pred[1024]{0:T(1024)(128)(4,1)S(1)} %add_compare_fusion.3, bf16[128,1,16,128]{3,0,2,1:T(8,128)(2,1)S(1)} %get-tuple-element.361, bf16[8,1024,2,1,128]{4,1,3,2,0:T(8,128)(2,1)} %get-tuple-element.358, s32[]{:T(128)S(6)} %select_n.118), kind=kOutput, calls=%fused_computation.1.clone.1 | convolution fusion | flops 543160320 | bytes 9184260 | tf_op jit(solution)/shard_map/while/body/eval_jaxpr/igqd,pgd->igqp/dot_general | solution.py:72
  185.9 5.8 %fusion.84 = f32[128,128,16]{1,0,2:T(8,128)S(1)} fusion(f32[1024,128,16]{1,0,2:T(8,128)} %get-tuple-element.316, f32[128,16]{0,1:T(8,128)S(1)} %max.47, pred[1024]{0:T(1024)(128)(4,1)S(1)} %add_compare_fusion.3, bf16[8,1024,2,1,128]{4,1,3,2,0:T(8,128)(2,1)} %get-tuple-element.358, s32[]{:T(128)S(6)} %select_n.118), kind=kOutput, calls=%fused_computation.8.clone.1 | convolution fusion | flops 547356672 | bytes 9709572 | tf_op jit(solution)/shard_map/while/body/eval_jaxpr/igqp,pgd->igqd/dot_general | solution.py:93
  191.7 2.5 fusion.85
  199.6 5.5 %bitcast_reduce_fusion.2 = (f32[128,16]{0,1:T(8,128)S(1)}, f32[1024,128,16]{1,0,2:T(8,128)}) fusion(pred[1024]{0:T(1024)(128)(4,1)S(1)} %add_compare_fusion.3, bf16[128,1,16,128]{3,0,2,1:T(8,128)(2,1)S(1)} %get-tuple-element.361, bf16[8,1024,2,1,128]{4,1,3,2,0:T(8,128)(2,1)} %get-tuple-element.358, s32[]{:T(128)S(6)} %select_n.118), kind=kOutput, calls=%fused_computation.1.clone.1 | convolution fusion | flops 543160320 | bytes 9184260 | tf_op jit(solution)/shard_map/while/body/eval_jaxpr/igqd,pgd->igqp/dot_general | solution.py:72
  205.9 5.8 %fusion.84 = f32[128,128,16]{1,0,2:T(8,128)S(1)} fusion(f32[1024,128,16]{1,0,2:T(8,128)} %get-tuple-element.316, f32[128,16]{0,1:T(8,128)S(1)} %max.47, pred[1024]{0:T(1024)(128)(4,1)S(1)} %add_compare_fusion.3, bf16[8,1024,2,1,128]{4,1,3,2,0:T(8,128)(2,1)} %get-tuple-element.358, s32[]{:T(128)S(6)} %select_n.118), kind=kOutput, calls=%fused_computation.8.clone.1 | convolution fusion | flops 547356672 | bytes 9709572 | tf_op jit(solution)/shard_map/while/body/eval_jaxpr/igqp,pgd->igqd/dot_general | solution.py:93
  211.8 2.5 fusion.85
  214.4 1.4 bitcast_dynamic-update-slice_fusion.5
  219.7 5.5 %bitcast_reduce_fusion.2 = (f32[128,16]{0,1:T(8,128)S(1)}, f32[1024,128,16]{1,0,2:T(8,128)}) fusion(pred[1024]{0:T(1024)(128)(4,1)S(1)} %add_compare_fusion.3, bf16[128,1,16,128]{3,0,2,1:T(8,128)(2,1)S(1)} %get-tuple-element.361, bf16[8,1024,2,1,128]{4,1,3,2,0:T(8,128)(2,1)} %get-tuple-element.358, s32[]{:T(128)S(6)} %select_n.118), kind=kOutput, calls=%fused_computation.1.clone.1 | convolution fusion | flops 543160320 | bytes 9184260 | tf_op jit(solution)/shard_map/while/body/eval_jaxpr/igqd,pgd->igqp/dot_general | solution.py:72
  226.0 5.8 %fusion.84 = f32[128,128,16]{1,0,2:T(8,128)S(1)} fusion(f32[1024,128,16]{1,0,2:T(8,128)} %get-tuple-element.316, f32[128,16]{0,1:T(8,128)S(1)} %max.47, pred[1024]{0:T(1024)(128)(4,1)S(1)} %add_compare_fusion.3, bf16[8,1024,2,1,128]{4,1,3,2,0:T(8,128)(2,1)} %get-tuple-element.358, s32[]{:T(128)S(6)} %select_n.118), kind=kOutput, calls=%fused_computation.8.clone.1 | convolution fusion | flops 547356672 | bytes 9709572 | tf_op jit(solution)/shard_map/while/body/eval_jaxpr/igqp,pgd->igqd/dot_general | solution.py:93
  231.8 2.5 fusion.85
  234.5 1.4 bitcast_dynamic-update-slice_fusion.5
  239.8 5.5 %bitcast_reduce_fusion.2 = (f32[128,16]{0,1:T(8,128)S(1)}, f32[1024,128,16]{1,0,2:T(8,128)}) fusion(pred[1024]{0:T(1024)(128)(4,1)S(1)} %add_compare_fusion.3, bf16[128,1,16,128]{3,0,2,1:T(8,128)(2,1)S(1)} %get-tuple-element.361, bf16[8,1024,2,1,128]{4,1,3,2,0:T(8,128)(2,1)} %get-tuple-element.358, s32[]{:T(128)S(6)} %select_n.118), kind=kOutput, calls=%fused_computation.1.clone.1 | convolution fusion | flops 543160320 | bytes 9184260 | tf_op jit(solution)/shard_map/while/body/eval_jaxpr/igqd,pgd->igqp/dot_general | solution.py:72
  246.0 5.8 %fusion.84 = f32[128,128,16]{1,0,2:T(8,128)S(1)} fusion(f32[1024,128,16]{1,0,2:T(8,128)} %get-tuple-element.316, f32[128,16]{0,1:T(8,128)S(1)} %max.47, pred[1024]{0:T(1024)(128)(4,1)S(1)} %add_compare_fusion.3, bf16[8,1024,2,1,128]{4,1,3,2,0:T(8,128)(2,1)} %get-tuple-element.358, s32[]{:T(128)S(6)} %select_n.118), kind=kOutput, calls=%fused_computation.8.clone.1 | convolution fusion | flops 547356672 | bytes 9709572 | tf_op jit(solution)/shard_map/while/body/eval_jaxpr/igqp,pgd->igqd/dot_general | solution.py:93
  251.9 2.5 fusion.85
  256.0 4.8 %multiply_reduce_fusion = f32[128,16,128]{0,2,1:T(8,128)S(1)} fusion(f32[8,128,16,128]{1,3,2,0:T(8,128)} %get-tuple-element.146, f32[8,128,16]{1,2,0:T(8,128)S(1)} %get-tuple-element.236), kind=kLoop, calls=%fused_computation.46 | loop fusion | flops 3932160 | bytes 9502720 | tf_op jit(solution)/shard_map/reduce_sum | solution.py:117
  262.7 5.2 %all-to-all-start.2 = ((f32[4,32,2080]{2,1,0:T(8,128)}), f32[4,32,2080]{2,1,0:T(8,128)S(1)}, u32[]{:S(2)}, u32[]{:S(2)}) async-start(f32[4,32,2080]{2,1,0:T(8,128)} %concatenate.17), calls=%async_computation.2 | async-start | bytes 2228224 | tf_op jit(solution)/shard_map/all_to_all | solution.py:121
  269.1 13.1 %all-to-all-done.2 = f32[4,32,2080]{2,1,0:T(8,128)S(1)} async-done(((f32[4,32,2080]{2,1,0:T(8,128)}), f32[4,32,2080]{2,1,0:T(8,128)S(1)}, u32[]{:S(2)}, u32[]{:S(2)}) %all-to-all-start.2) | async-done | bytes 1064992 | tf_op jit(solution)/shard_map/all_to_all | solution.py:121
  (142 shorter events, 24.1 us)
Async XLA Ops:
  0.0 88.8 %copy-start = (bf16[32,128]{1,0:T(8,128)(2,1)S(1)}, bf16[32,128]{1,0:T(8,128)(2,1)}, u32[]{:S(2)}) copy-start(bf16[32,128]{1,0:T(8,128)(2,1)} %param.13) | copy-start | bytes 24580
  10.6 20.0 %all-to-all-start.1 = ((bf16[8,4,2048]{2,1,0:T(4,128)(2,1)}), bf16[8,4,2048]{2,1,0:T(4,128)(2,1)S(1)}, u32[]{:S(2)}, u32[]{:S(2)}) async-start(bf16[8,4,2048]{2,1,0:T(4,128)(2,1)} %constant_dynamic-update-slice_fusion), calls=%async_computation.1 | async-start | bytes 262144 | tf_op jit(solution)/shard_map/all_to_all | solution.py:46
  26.5 10.9 %copy-start.3 = (s32[8]{0:T(128)S(1)}, s32[8]{0:T(128)}, u32[]{:S(2)}) copy-start(s32[8]{0:T(128)} %param.17) | copy-start | bytes 100
  26.5 11.5 %copy-start.2 = (s32[8,128]{1,0:T(8,128)S(1)}, s32[8,128]{1,0:T(8,128)}, u32[]{:S(2)}) copy-start(s32[8,128]{1,0:T(8,128)} %param.15) | copy-start | bytes 12292
  30.7 58.3 %all-to-all-start = ((bf16[8,1024,256]{1,2,0:T(8,128)(2,1)}), bf16[8,1024,256]{1,2,0:T(8,128)(2,1)}, u32[]{:S(2)}, u32[]{:S(2)}) async-start(bf16[8,1024,256]{1,2,0:T(8,128)(2,1)} %pad_maximum_fusion), calls=%async_computation | async-start | bytes 8388608 | tf_op jit(solution)/shard_map/all_to_all | solution.py:54
  37.3 58.1 %copy-start.1 = (bf16[32,128]{1,0:T(8,128)(2,1)S(1)}, bf16[32,128]{1,0:T(8,128)(2,1)}, u32[]{:S(2)}) copy-start(bf16[32,128]{1,0:T(8,128)(2,1)} %param.14) | copy-start | bytes 24580
  105.6 5.9 %slice-start = ((s8[8388608]{0:T(1024)(128)(4,1)}), s8[4194304]{0:T(1024)(128)(4,1)S(1)}, s32[]{:S(2)}) async-start(s8[8388608]{0:T(1024)(128)(4,1)} %bitcast.176), calls=%async_computation.3 | async-start | bytes 8388608 | tf_op jit(solution)/shard_map/while
  105.7 5.9 %slice-start.1 = ((s8[8388608]{0:T(1024)(128)(4,1)}), s8[4194304]{0:T(1024)(128)(4,1)S(1)}, s32[]{:S(2)}) async-start(s8[8388608]{0:T(1024)(128)(4,1)} %bitcast.176), calls=%async_computation.4 | async-start | bytes 8388608 | tf_op jit(solution)/shard_map/while
  125.6 5.9 %slice-start = ((s8[8388608]{0:T(1024)(128)(4,1)}), s8[4194304]{0:T(1024)(128)(4,1)S(1)}, s32[]{:S(2)}) async-start(s8[8388608]{0:T(1024)(128)(4,1)} %bitcast.176), calls=%async_computation.3 | async-start | bytes 8388608 | tf_op jit(solution)/shard_map/while
  125.7 5.9 %slice-start.1 = ((s8[8388608]{0:T(1024)(128)(4,1)}), s8[4194304]{0:T(1024)(128)(4,1)S(1)}, s32[]{:S(2)}) async-start(s8[8388608]{0:T(1024)(128)(4,1)} %bitcast.176), calls=%async_computation.4 | async-start | bytes 8388608 | tf_op jit(solution)/shard_map/while
  145.7 5.9 %slice-start = ((s8[8388608]{0:T(1024)(128)(4,1)}), s8[4194304]{0:T(1024)(128)(4,1)S(1)}, s32[]{:S(2)}) async-start(s8[8388608]{0:T(1024)(128)(4,1)} %bitcast.176), calls=%async_computation.3 | async-start | bytes 8388608 | tf_op jit(solution)/shard_map/while
  145.8 5.9 %slice-start.1 = ((s8[8388608]{0:T(1024)(128)(4,1)}), s8[4194304]{0:T(1024)(128)(4,1)S(1)}, s32[]{:S(2)}) async-start(s8[8388608]{0:T(1024)(128)(4,1)} %bitcast.176), calls=%async_computation.4 | async-start | bytes 8388608 | tf_op jit(solution)/shard_map/while
  165.7 5.9 %slice-start = ((s8[8388608]{0:T(1024)(128)(4,1)}), s8[4194304]{0:T(1024)(128)(4,1)S(1)}, s32[]{:S(2)}) async-start(s8[8388608]{0:T(1024)(128)(4,1)} %bitcast.176), calls=%async_computation.3 | async-start | bytes 8388608 | tf_op jit(solution)/shard_map/while
  165.8 5.9 %slice-start.1 = ((s8[8388608]{0:T(1024)(128)(4,1)}), s8[4194304]{0:T(1024)(128)(4,1)S(1)}, s32[]{:S(2)}) async-start(s8[8388608]{0:T(1024)(128)(4,1)} %bitcast.176), calls=%async_computation.4 | async-start | bytes 8388608 | tf_op jit(solution)/shard_map/while
  185.8 5.9 %slice-start = ((s8[8388608]{0:T(1024)(128)(4,1)}), s8[4194304]{0:T(1024)(128)(4,1)S(1)}, s32[]{:S(2)}) async-start(s8[8388608]{0:T(1024)(128)(4,1)} %bitcast.176), calls=%async_computation.3 | async-start | bytes 8388608 | tf_op jit(solution)/shard_map/while
  185.9 5.9 %slice-start.1 = ((s8[8388608]{0:T(1024)(128)(4,1)}), s8[4194304]{0:T(1024)(128)(4,1)S(1)}, s32[]{:S(2)}) async-start(s8[8388608]{0:T(1024)(128)(4,1)} %bitcast.176), calls=%async_computation.4 | async-start | bytes 8388608 | tf_op jit(solution)/shard_map/while
  205.8 5.9 %slice-start = ((s8[8388608]{0:T(1024)(128)(4,1)}), s8[4194304]{0:T(1024)(128)(4,1)S(1)}, s32[]{:S(2)}) async-start(s8[8388608]{0:T(1024)(128)(4,1)} %bitcast.176), calls=%async_computation.3 | async-start | bytes 8388608 | tf_op jit(solution)/shard_map/while
  205.9 5.9 %slice-start.1 = ((s8[8388608]{0:T(1024)(128)(4,1)}), s8[4194304]{0:T(1024)(128)(4,1)S(1)}, s32[]{:S(2)}) async-start(s8[8388608]{0:T(1024)(128)(4,1)} %bitcast.176), calls=%async_computation.4 | async-start | bytes 8388608 | tf_op jit(solution)/shard_map/while
  225.9 5.9 %slice-start = ((s8[8388608]{0:T(1024)(128)(4,1)}), s8[4194304]{0:T(1024)(128)(4,1)S(1)}, s32[]{:S(2)}) async-start(s8[8388608]{0:T(1024)(128)(4,1)} %bitcast.176), calls=%async_computation.3 | async-start | bytes 8388608 | tf_op jit(solution)/shard_map/while
  226.0 5.9 %slice-start.1 = ((s8[8388608]{0:T(1024)(128)(4,1)}), s8[4194304]{0:T(1024)(128)(4,1)S(1)}, s32[]{:S(2)}) async-start(s8[8388608]{0:T(1024)(128)(4,1)} %bitcast.176), calls=%async_computation.4 | async-start | bytes 8388608 | tf_op jit(solution)/shard_map/while
  245.9 5.9 %slice-start = ((s8[8388608]{0:T(1024)(128)(4,1)}), s8[4194304]{0:T(1024)(128)(4,1)S(1)}, s32[]{:S(2)}) async-start(s8[8388608]{0:T(1024)(128)(4,1)} %bitcast.176), calls=%async_computation.3 | async-start | bytes 8388608 | tf_op jit(solution)/shard_map/while
  246.0 5.9 %slice-start.1 = ((s8[8388608]{0:T(1024)(128)(4,1)}), s8[4194304]{0:T(1024)(128)(4,1)S(1)}, s32[]{:S(2)}) async-start(s8[8388608]{0:T(1024)(128)(4,1)} %bitcast.176), calls=%async_computation.4 | async-start | bytes 8388608 | tf_op jit(solution)/shard_map/while
  256.0 11.9 %copy-start.4 = (s32[8]{0:T(128)S(1)}, s32[8]{0:T(128)}, u32[]{:S(2)}) copy-start(s32[8]{0:T(128)} %param.16) | copy-start | bytes 100
  262.7 19.5 %all-to-all-start.2 = ((f32[4,32,2080]{2,1,0:T(8,128)}), f32[4,32,2080]{2,1,0:T(8,128)S(1)}, u32[]{:S(2)}, u32[]{:S(2)}) async-start(f32[4,32,2080]{2,1,0:T(8,128)} %concatenate.17), calls=%async_computation.2 | async-start | bytes 2228224 | tf_op jit(solution)/shard_map/all_to_all | solution.py:121
